TPU v7x, 512 devices: a whole 4x4x16 slice. The times are simulated.
512 devices in a mesh: event: 8 (over y, core), tile: 64 (over x, z).
Axes of the slice: x: 4, y: 4, z: 16, core: 2. Of those that a mesh axis runs over, the one named last changes fastest.
Arguments:
- surface_start: float32 [8, 512, 8192], P('event', 'tile'), may hold values from -6 to 6
- east_start: float32 [8, 512, 8192], P('event', 'tile'), may hold values from -5 to 5
- north_start: float32 [8, 512, 8192], P('event', 'tile'), may hold values from -5 to 5
- still_depth: float32 [512, 8192], P('tile'), may hold values from 1 to 4
- roughness: float32 [512, 8192], P('tile'), may hold values from 0.5 to 2
- wet_masks: int32 [8, 2, 512, 8192], P('event', None, 'tile'), may hold values 0 or 1
- gauge_tiles: int32 [8, 16384, 1], P('event', 'tile'), may hold values from 0 to 63; in each aligned block of 256 rows (0 to 255, 256 to 511, ..., all dimensions but the last counted through in order) at most 8 rows name the same one
- gauge_cells: int32 [8, 16384], P('event', 'tile'), may hold values from 0 to 65535
- gauge_values: float32 [8, 16384], P('event', 'tile'), may hold values from -6 to 6
- survey_surface: float32 [8, 512, 8192], P('event', 'tile'), may hold values from -6 to 6
Outputs:
- roughness_grad: float32 [512, 8192], P('tile', 'event')
Inputs may be any that keep to these rules, and one draw needn't show every extreme that they name: `gauge_tiles`: of the gauges of one event listed on one strip, at most 8 lie in any one strip, and some strip receives exactly 8.
All inputs are finite; a program needn't handle non-finite values. No bound on the sum of `wet_masks` on one device may be relied on, other than what follows from the above.
Results may differ from a plain program's by a relative error of at most 0.0003.
Values sent between devices are 32-bit elements; how exact they have to be, the bound alone decides.
No kernel may reach another device: no remote copies, remote signals or barrier semaphores. Data moves between devices by JAX's collectives and lax.ppermute only.
A program may use at most 64 MiB of HBM per device.

v0:
```python
import jax
import jax.numpy as jnp
from jax import lax
from jax.sharding import PartitionSpec as P

STEPS = 2


def shifted(value, axis, steps):
    count = lax.axis_size(axis)
    initial, last = (max(0, -steps), min(count, count - steps))
    return lax.ppermute(value, axis, [(source, source + steps) for source in range(initial, last)])


def padded_2(cells, sides, width):
    for axis, dim in sides:
        count = lax.axis_size(axis)
        ends = count - 1
        head = lax.slice_in_dim(cells, 0, width, axis=dim)
        tail = lax.slice_in_dim(cells, cells.shape[dim] - width, cells.shape[dim], axis=dim)
        cells = jnp.concatenate(
            [
                lax.ppermute(tail, axis, [(i, (i + 1) % count) for i in range(ends)]),
                cells,
                lax.ppermute(head, axis, [((i + 1) % count, i) for i in range(ends)]),
            ],
            axis=dim,
        )
    return cells


def interior(field):
    return field[1:-1]


def across(field):
    padded = jnp.pad(field, ((0, 0), (1, 1)))
    return padded[:, 2:] - padded[:, :-2]


def along(field):
    return field[2:] - field[:-2]


def advance(surface, east, north, depth_rows, rough_rows, wetness):
    depth_inner = interior(depth_rows)
    depth_safe = jnp.where(depth_inner > 0, depth_inner, 1.0)
    east_inner = interior(east)
    north_inner = interior(north)
    speed = jnp.sqrt(east_inner * east_inner + north_inner * north_inner + 1.0)
    rough_inner = interior(rough_rows)
    friction = 1.0 + 2.0 * rough_inner * rough_inner * speed / depth_safe ** (4.0 / 3.0)
    wet_inner = interior(wetness)
    new_east = wet_inner * (east_inner - 0.2 * depth_inner * across(interior(surface))) / friction
    new_north = wet_inner * (north_inner - 0.2 * depth_inner * along(surface)) / friction
    new_surface = interior(interior(surface)) - 0.25 * interior(wet_inner) * (
        interior(across(new_east)) + along(new_north)
    )
    return (new_surface, interior(new_east), interior(new_north))


def fold_rims(stacked, width):
    upper = stacked[:, :width]
    lower = stacked[:, stacked.shape[1] - width :]
    inner = stacked[:, width : stacked.shape[1] - width]
    from_below = shifted(upper, "tile", -1)
    from_above = shifted(lower, "tile", 1)
    inner = inner.at[:, inner.shape[1] - width :].add(from_below)
    return inner.at[:, :width].add(from_above)


def per_device(
    surface_start,
    east_start,
    north_start,
    still_depth,
    roughness,
    wet_masks,
    gauge_tiles,
    gauge_cells,
    gauge_values,
    survey_surface,
):
    row_count, col_count = still_depth.shape
    wet_float = wet_masks[0].astype(jnp.float32)
    statics = jnp.stack((still_depth, roughness))
    stored = []
    width = 2
    static_pad = padded_2(statics, (("tile", 1),), 2)
    surface, east, north = (surface_start[0], east_start[0], north_start[0])
    for step_index in range(STEPS):
        padded = padded_2(
            jnp.stack((surface, east, north, wet_float[step_index])), (("tile", 1),), 2
        )
        record = (padded[0], padded[1], padded[2], static_pad[0], static_pad[1], padded[3])
        stored.append(record)
        surface, east, north = advance(*record)
    strip_tiles = gauge_tiles[0, :, 0]
    tile_count = lax.axis_size("tile")
    listed = strip_tiles.shape[0]
    capacity = max(2, 2 * listed // tile_count)
    onehot = (strip_tiles[:, None] == jnp.arange(tile_count, dtype=jnp.int32)[None, :]).astype(
        jnp.int32
    )
    before = jnp.cumsum(onehot, axis=0) - onehot
    rank = jnp.sum(onehot * before, axis=1)
    slot = strip_tiles * capacity + rank
    cell_count = row_count * col_count
    send_cells = (
        jnp.full((tile_count * capacity,), cell_count, jnp.int32).at[slot].set(gauge_cells[0])
    )
    send_values = jnp.zeros((tile_count * capacity,), jnp.float32).at[slot].set(gauge_values[0])
    got_cells, got_values = (
        lax.all_to_all(
            send_cells.reshape(tile_count, capacity),
            "tile",
            split_axis=0,
            concat_axis=0,
            tiled=True,
        ),
        lax.all_to_all(
            send_values.reshape(tile_count, capacity),
            "tile",
            split_axis=0,
            concat_axis=0,
            tiled=True,
        ),
    )
    flat_cells = got_cells.reshape(-1)
    valid = flat_cells < cell_count
    seen = jnp.take(surface.reshape(-1), flat_cells, mode="fill", fill_value=0.0)
    missing = jnp.where(valid, seen - got_values.reshape(-1), 0.0)
    gauge_sense = (
        jnp.zeros((cell_count,), jnp.float32)
        .at[flat_cells]
        .add(missing, mode="drop")
        .reshape(row_count, col_count)
    )
    sense_surface = gauge_sense + (surface - survey_surface[0])
    sense_east = jnp.zeros_like(sense_surface)
    sense_north = jnp.zeros_like(sense_surface)
    rough_sense = jnp.zeros((row_count + 2 * width, col_count), jnp.float32)
    for step_index in reversed(range(STEPS)):
        surface_in, east_in, north_in, depth_rows, rough_rows, wetness = stored[step_index]

        def local_step(surface_arg, east_arg, north_arg, rough_arg):
            return advance(surface_arg, east_arg, north_arg, depth_rows, rough_arg, wetness)

        outputs, pullback = jax.vjp(local_step, surface_in, east_in, north_in, rough_rows)
        back_surface, back_east, back_north, back_rough = pullback(
            (sense_surface, sense_east, sense_north)
        )
        rough_sense = rough_sense + back_rough
        if step_index > 0:
            folded = fold_rims(jnp.stack((back_surface, back_east, back_north)), 2)
            sense_surface, sense_east, sense_north = (folded[0], folded[1], folded[2])
    local_grad = fold_rims(rough_sense[None], width)[0]
    total = lax.psum(local_grad, "event")
    share = col_count // lax.axis_size("event")
    return lax.dynamic_slice_in_dim(total, lax.axis_index("event") * share, share, 1)


def solution(mesh):
    placed = (
        P("event", "tile", None),
        P("event", "tile", None),
        P("event", "tile", None),
        P("tile", None),
        P("tile", None),
        P("event", None, "tile", None),
        P("event", "tile", None),
        P("event", "tile"),
        P("event", "tile"),
        P("event", "tile", None),
    )
    return jax.shard_map(
        per_device, mesh=mesh, in_specs=placed, out_specs=P("tile", "event"), check_vma=False
    )
```

profile of v0, /device:TPU:2, one launch (start us, length us, event | category | flops | bytes accessed | tf_op | source)
XLA Modules:
  0.0 217.5 jit_solution(9492636156233918174)
XLA Ops:
  6.5 1.4 pad_maximum_fusion.31
  7.9 3.8 %collective-permute-start = (f32[2,2,8192]{2,1,0:T(2,128)S(1)}, f32[2,2,8192]{2,1,0:T(2,128)S(1)}, u32[]{:S(2)}, u32[]{:S(2)}) collective-permute-start(f32[2,2,8192]{2,1,0:T(2,128)S(1)} %get-tuple-element.102), channel_id=1, source_target_pairs={{0,1},{1,2},{2,3},{3,4},{4,5},{5,6},{6,7},{7,8},{8,9},{9,10},{10,1... | collective-permute-start | bytes 393224 | tf_op jit(solution)/shard_map/ppermute | solution.py:23
  11.7 9.5 %collective-permute-start.1 = (f32[2,2,8192]{2,1,0:T(2,128)S(1)}, f32[2,2,8192]{2,1,0:T(2,128)}, u32[]{:S(2)}, u32[]{:S(2)}) collective-permute-start(f32[2,2,8192]{2,1,0:T(2,128)S(1)} %get-tuple-element.103), channel_id=1, source_target_pairs={{1,0},{2,1},{3,2},{4,3},{5,4},{6,5},{7,6},{8,7},{9,8},{10,9},{11,1... | collective-permute-start | bytes 393224 | tf_op jit(solution)/shard_map/ppermute | solution.py:25
  21.2 0.7 fusion.44
  22.7 0.8 fusion.40
  24.2 1.6 scatter_custom_fusion
  25.8 0.7 all_to_all.12
  26.5 12.4 %all-to-all-start = ((s32[64,1,8]{2,1,0:T(1,128)}), s32[64,1,8]{2,1,0:T(1,128)S(1)}, u32[]{:S(2)}, u32[]{:S(2)}) async-start(s32[64,1,8]{2,1,0:T(1,128)} %bitcast.12), calls=%async_computation | async-start | bytes 65536 | tf_op jit(solution)/shard_map/all_to_all | solution.py:114
  38.9 1.1 convert_element_type.19
  40.0 1.6 scatter_custom_fusion.1
  41.6 0.7 all_to_all.14
  42.3 10.1 %all-to-all-done = s32[64,1,8]{2,1,0:T(1,128)S(1)} async-done(((s32[64,1,8]{2,1,0:T(1,128)}), s32[64,1,8]{2,1,0:T(1,128)S(1)}, u32[]{:S(2)}, u32[]{:S(2)}) %all-to-all-start) | async-done | bytes 2080 | tf_op jit(solution)/shard_map/all_to_all | solution.py:114
  52.4 5.5 %all-to-all-start.1 = ((f32[64,1,8]{2,1,0:T(1,128)}), f32[64,1,8]{2,1,0:T(1,128)S(1)}, u32[]{:S(2)}, u32[]{:S(2)}) async-start(f32[64,1,8]{2,1,0:T(1,128)} %bitcast.32), calls=%async_computation.1 | async-start | bytes 65536 | tf_op jit(solution)/shard_map/all_to_all | solution.py:121
  57.9 1.0 pad_maximum_fusion.27
  58.9 3.4 %collective-permute-start.2 = (f32[4,2,8192]{2,1,0:T(2,128)}, f32[4,2,8192]{2,1,0:T(2,128)S(1)}, u32[]{:S(2)}, u32[]{:S(2)}) collective-permute-start(f32[4,2,8192]{2,1,0:T(2,128)} %get-tuple-element.88), channel_id=1, source_target_pairs={{0,1},{1,2},{2,3},{3,4},{4,5},{5,6},{6,7},{7,8},{8,9},{9,10},{10,1... | collective-permute-start | bytes 786440 | tf_op jit(solution)/shard_map/ppermute | solution.py:23
  62.2 4.6 %collective-permute-start.3 = (f32[4,2,8192]{2,1,0:T(2,128)}, f32[4,2,8192]{2,1,0:T(2,128)S(1)}, u32[]{:S(2)}, u32[]{:S(2)}) collective-permute-start(f32[4,2,8192]{2,1,0:T(2,128)} %get-tuple-element.89), channel_id=1, source_target_pairs={{1,0},{2,1},{3,2},{4,3},{5,4},{6,5},{7,6},{8,7},{9,8},{10,9},{11,1... | collective-permute-start | bytes 786440 | tf_op jit(solution)/shard_map/ppermute | solution.py:25
  67.4 0.7 reduce.18
  68.3 3.0 %all-to-all-done.1 = f32[64,1,8]{2,1,0:T(1,128)S(1)} async-done(((f32[64,1,8]{2,1,0:T(1,128)}), f32[64,1,8]{2,1,0:T(1,128)S(1)}, u32[]{:S(2)}, u32[]{:S(2)}) %all-to-all-start.1) | async-done | bytes 2080 | tf_op jit(solution)/shard_map/all_to_all | solution.py:121
  71.9 0.7 reduce.19
  72.7 1.3 pad_maximum_fusion.3
  74.7 0.7 copy-done.20
  75.8 2.0 fusion.58
  77.9 1.4 pad_slice_fusion.3
  79.6 2.6 %collective-permute-start.4 = (f32[4,2,8192]{2,1,0:T(2,128)S(1)}, f32[4,2,8192]{2,1,0:T(2,128)S(1)}, u32[]{:S(2)}, u32[]{:S(2)}) collective-permute-start(f32[4,2,8192]{2,1,0:T(2,128)S(1)} %get-tuple-element.86), channel_id=1, source_target_pairs={{0,1},{1,2},{2,3},{3,4},{4,5},{5,6},{6,7},{7,8},{8,9},{9,10},{10,1... | collective-permute-start | bytes 786440 | tf_op jit(solution)/shard_map/ppermute | solution.py:23
  82.2 5.5 %collective-permute-start.5 = (f32[4,2,8192]{2,1,0:T(2,128)S(1)}, f32[4,2,8192]{2,1,0:T(2,128)S(1)}, u32[]{:S(2)}, u32[]{:S(2)}) collective-permute-start(f32[4,2,8192]{2,1,0:T(2,128)S(1)} %get-tuple-element.87), channel_id=1, source_target_pairs={{1,0},{2,1},{3,2},{4,3},{5,4},{6,5},{7,6},{8,7},{9,8},{10,9},{11,1... | collective-permute-start | bytes 786440 | tf_op jit(solution)/shard_map/ppermute | solution.py:25
  87.8 2.2 %collective-permute-done.4 = f32[4,2,8192]{2,1,0:T(2,128)S(1)} collective-permute-done((f32[4,2,8192]{2,1,0:T(2,128)S(1)}, f32[4,2,8192]{2,1,0:T(2,128)S(1)}, u32[]{:S(2)}, u32[]{:S(2)}) %collective-permute-start.4) | collective-permute-done | bytes 262176 | tf_op jit(solution)/shard_map/ppermute | solution.py:23
  90.0 1.5 collective-permute-done.5
  91.8 2.0 fusion.55
  94.2 1.1 fusion.56
  95.3 0.8 fusion.29
  96.1 1.0 copy.16
  97.1 3.1 %gather_fusion = f32[512]{0:T(512)S(1)} fusion(f32[65536]{0:T(1024)S(1)} %bitcast.247, s32[1024]{0:T(1024)S(1)} %pad_clamp_fusion), kind=kCustom, calls=%fused_computation | custom fusion | bytes 6144 | tf_op jit(solution)/shard_map/jit(_take)/gather | solution.py:131
  100.3 3.9 %scatter_custom_fusion.2 = f32[65536]{0:T(1024)} fusion(s32[512]{0:T(512)S(1)} %bitcast.260, f32[512]{0:T(512)S(1)} %subtract_select_fusion, f32[]{:T(128)} %constant.144.clone.1), kind=kCustom, calls=%fused_computation.127 | custom fusion | flops 512 | bytes 262148 | tf_op jit(solution)/shard_map/scatter-add | solution.py:136
  104.2 1.0 reshape.257
  105.3 1.3 fusion.53
  106.8 1.7 fusion
  108.6 0.7 add_add_fusion.1
  110.2 6.5 %collective-permute-start.6 = (f32[3,2,8192]{2,1,0:T(2,128)S(1)}, f32[3,2,8192]{2,1,0:T(2,128)S(1)}, u32[]{:S(2)}, u32[]{:S(2)}) collective-permute-start(f32[3,2,8192]{2,1,0:T(2,128)S(1)} %get-tuple-element.85), channel_id=1, source_target_pairs={{1,0},{2,1},{3,2},{4,3},{5,4},{6,5},{7,6},{8,7},{9,8},{10,9},{11,1... | collective-permute-start | bytes 589832 | tf_op jit(solution)/shard_map/ppermute | solution.py:12
  116.9 2.1 collective-permute-start.7
  119.0 0.9 collective-permute-done.6
  120.1 6.6 %collective-permute-done.7 = f32[3,2,8192]{2,1,0:T(2,128)S(1)} collective-permute-done((f32[3,2,8192]{2,1,0:T(2,128)S(1)}, f32[3,2,8192]{2,1,0:T(2,128)S(1)}, u32[]{:S(2)}, u32[]{:S(2)}) %collective-permute-start.7) | collective-permute-done | bytes 196640 | tf_op jit(solution)/shard_map/ppermute | solution.py:12
  127.1 1.5 fusion.1
  128.9 1.9 collective-permute-start.8
  130.8 3.9 %collective-permute-start.9 = (f32[1,2,8192]{2,1,0:T(2,128)S(1)}, f32[1,2,8192]{2,1,0:T(2,128)S(1)}, u32[]{:S(2)}, u32[]{:S(2)}) collective-permute-start(f32[1,2,8192]{2,1,0:T(2,128)S(1)} %get-tuple-element.92), channel_id=1, source_target_pairs={{0,1},{1,2},{2,3},{3,4},{4,5},{5,6},{6,7},{7,8},{8,9},{9,10},{10,1... | collective-permute-start | bytes 196616 | tf_op jit(solution)/shard_map/ppermute | solution.py:12
  135.1 4.0 %collective-permute-done.9 = f32[1,2,8192]{2,1,0:T(2,128)S(1)} collective-permute-done((f32[1,2,8192]{2,1,0:T(2,128)S(1)}, f32[1,2,8192]{2,1,0:T(2,128)S(1)}, u32[]{:S(2)}, u32[]{:S(2)}) %collective-permute-start.9) | collective-permute-done | bytes 65568 | tf_op jit(solution)/shard_map/ppermute | solution.py:12
  139.2 0.7 copy-done.22
  139.9 69.4 %all-reduce.30.cloned.1.call-done = f32[8,8192]{1,0:T(8,128)} async-done(((f32[8,8192]{1,0:T(8,128)}), f32[8,8192]{1,0:T(8,128)}) %all-reduce.30.cloned.1.call-update) | async-done | bytes 262160 | tf_op jit(solution)/shard_map/psum | solution.py:158
  209.3 1.4 constant_dynamic-slice_fusion
  (95 shorter events, 7.7 us)
Async XLA Ops:
  6.5 51.3 %copy-start.9 = (f32[1,8,8192]{2,1,0:T(8,128)S(1)}, f32[1,8,8192]{2,1,0:T(8,128)}, u32[]{:S(2)}) copy-start(f32[1,8,8192]{2,1,0:T(8,128)} %param.18) | copy-start | bytes 786436
  6.5 51.3 %copy-start.12 = (f32[1,8,8192]{2,1,0:T(8,128)S(1)}, f32[1,8,8192]{2,1,0:T(8,128)}, u32[]{:S(2)}) copy-start(f32[1,8,8192]{2,1,0:T(8,128)} %param.19) | copy-start | bytes 786436
  6.5 51.4 %copy-start.10 = (f32[1,8,8192]{2,1,0:T(8,128)S(1)}, f32[1,8,8192]{2,1,0:T(8,128)}, u32[]{:S(2)}) copy-start(f32[1,8,8192]{2,1,0:T(8,128)} %param.20) | copy-start | bytes 786436
  7.9 64.8 %collective-permute-start = (f32[2,2,8192]{2,1,0:T(2,128)S(1)}, f32[2,2,8192]{2,1,0:T(2,128)S(1)}, u32[]{:S(2)}, u32[]{:S(2)}) collective-permute-start(f32[2,2,8192]{2,1,0:T(2,128)S(1)} %get-tuple-element.102), channel_id=1, source_target_pairs={{0,1},{1,2},{2,3},{3,4},{4,5},{5,6},{6,7},{7,8},{8,9},{9,10},{10,1... | collective-permute-start | bytes 393224 | tf_op jit(solution)/shard_map/ppermute | solution.py:23
  11.7 61.0 %collective-permute-start.1 = (f32[2,2,8192]{2,1,0:T(2,128)S(1)}, f32[2,2,8192]{2,1,0:T(2,128)}, u32[]{:S(2)}, u32[]{:S(2)}) collective-permute-start(f32[2,2,8192]{2,1,0:T(2,128)S(1)} %get-tuple-element.103), channel_id=1, source_target_pairs={{1,0},{2,1},{3,2},{4,3},{5,4},{6,5},{7,6},{8,7},{9,8},{10,9},{11,1... | collective-permute-start | bytes 393224 | tf_op jit(solution)/shard_map/ppermute | solution.py:25
  26.5 25.9 %all-to-all-start = ((s32[64,1,8]{2,1,0:T(1,128)}), s32[64,1,8]{2,1,0:T(1,128)S(1)}, u32[]{:S(2)}, u32[]{:S(2)}) async-start(s32[64,1,8]{2,1,0:T(1,128)} %bitcast.12), calls=%async_computation | async-start | bytes 65536 | tf_op jit(solution)/shard_map/all_to_all | solution.py:114
  40.0 39.3 %copy-start.2 = (f32[1,2,8,8192]{3,2,1,0:T(8,128)}, f32[1,2,8,8192]{3,2,1,0:T(8,128)S(1)}, u32[]{:S(2)}) copy-start(f32[1,2,8,8192]{3,2,1,0:T(8,128)S(1)} %convert_element_type.19) | copy-start | bytes 1572868
  52.4 19.0 %all-to-all-start.1 = ((f32[64,1,8]{2,1,0:T(1,128)}), f32[64,1,8]{2,1,0:T(1,128)S(1)}, u32[]{:S(2)}, u32[]{:S(2)}) async-start(f32[64,1,8]{2,1,0:T(1,128)} %bitcast.32), calls=%async_computation.1 | async-start | bytes 65536 | tf_op jit(solution)/shard_map/all_to_all | solution.py:121
  57.8 151.5 %all-reduce.30.cloned.1.call-start = ((), (), s32[]{:S(2)}) async-start(), calls=%async_computation.2 | async-start | bytes 524288 | tf_op jit(solution)/shard_map/psum | solution.py:158
  58.9 15.1 %collective-permute-start.2 = (f32[4,2,8192]{2,1,0:T(2,128)}, f32[4,2,8192]{2,1,0:T(2,128)S(1)}, u32[]{:S(2)}, u32[]{:S(2)}) collective-permute-start(f32[4,2,8192]{2,1,0:T(2,128)} %get-tuple-element.88), channel_id=1, source_target_pairs={{0,1},{1,2},{2,3},{3,4},{4,5},{5,6},{6,7},{7,8},{8,9},{9,10},{10,1... | collective-permute-start | bytes 786440 | tf_op jit(solution)/shard_map/ppermute | solution.py:23
  62.2 11.8 %collective-permute-start.3 = (f32[4,2,8192]{2,1,0:T(2,128)}, f32[4,2,8192]{2,1,0:T(2,128)S(1)}, u32[]{:S(2)}, u32[]{:S(2)}) collective-permute-start(f32[4,2,8192]{2,1,0:T(2,128)} %get-tuple-element.89), channel_id=1, source_target_pairs={{1,0},{2,1},{3,2},{4,3},{5,4},{6,5},{7,6},{8,7},{9,8},{10,9},{11,1... | collective-permute-start | bytes 786440 | tf_op jit(solution)/shard_map/ppermute | solution.py:25
  74.0 0.7 copy-start.18
  74.7 0.7 copy-start.20
  75.7 2.1 copy-start
  75.8 2.1 copy-start.11
  75.8 2.1 copy-start.13
  75.8 2.1 copy-start.19
  75.8 2.1 copy-start.21
  77.8 1.5 copy-start.7
  79.6 10.4 %collective-permute-start.4 = (f32[4,2,8192]{2,1,0:T(2,128)S(1)}, f32[4,2,8192]{2,1,0:T(2,128)S(1)}, u32[]{:S(2)}, u32[]{:S(2)}) collective-permute-start(f32[4,2,8192]{2,1,0:T(2,128)S(1)} %get-tuple-element.86), channel_id=1, source_target_pairs={{0,1},{1,2},{2,3},{3,4},{4,5},{5,6},{6,7},{7,8},{8,9},{9,10},{10,1... | collective-permute-start | bytes 786440 | tf_op jit(solution)/shard_map/ppermute | solution.py:23
  82.2 9.2 %collective-permute-start.5 = (f32[4,2,8192]{2,1,0:T(2,128)S(1)}, f32[4,2,8192]{2,1,0:T(2,128)S(1)}, u32[]{:S(2)}, u32[]{:S(2)}) collective-permute-start(f32[4,2,8192]{2,1,0:T(2,128)S(1)} %get-tuple-element.87), channel_id=1, source_target_pairs={{1,0},{2,1},{3,2},{4,3},{5,4},{6,5},{7,6},{8,7},{9,8},{10,9},{11,1... | collective-permute-start | bytes 786440 | tf_op jit(solution)/shard_map/ppermute | solution.py:25
  93.9 1.4 copy-start.5
  94.2 1.1 copy-start.3
  105.2 1.4 copy-start.6
  105.2 1.4 copy-start.16
  105.3 1.6 copy-start.17
  110.2 9.7 %collective-permute-start.6 = (f32[3,2,8192]{2,1,0:T(2,128)S(1)}, f32[3,2,8192]{2,1,0:T(2,128)S(1)}, u32[]{:S(2)}, u32[]{:S(2)}) collective-permute-start(f32[3,2,8192]{2,1,0:T(2,128)S(1)} %get-tuple-element.85), channel_id=1, source_target_pairs={{1,0},{2,1},{3,2},{4,3},{5,4},{6,5},{7,6},{8,7},{9,8},{10,9},{11,1... | collective-permute-start | bytes 589832 | tf_op jit(solution)/shard_map/ppermute | solution.py:12
  116.8 10.1 %copy-start.4 = (f32[1,2,8,8192]{3,2,1,0:T(8,128)S(1)}, f32[1,2,8,8192]{3,2,1,0:T(8,128)}, u32[]{:S(2)}) copy-start(f32[1,2,8,8192]{3,2,1,0:T(8,128)} %copy-done.2) | copy-start | bytes 1572868
  116.9 9.8 %collective-permute-start.7 = (f32[3,2,8192]{2,1,0:T(2,128)S(1)}, f32[3,2,8192]{2,1,0:T(2,128)S(1)}, u32[]{:S(2)}, u32[]{:S(2)}) collective-permute-start(f32[3,2,8192]{2,1,0:T(2,128)S(1)} %get-tuple-element.84), channel_id=1, source_target_pairs={{0,1},{1,2},{2,3},{3,4},{4,5},{5,6},{6,7},{7,8},{8,9},{9,10},{10,1... | collective-permute-start | bytes 589832 | tf_op jit(solution)/shard_map/ppermute | solution.py:12
  120.1 7.0 %copy-start.1 = (f32[4,12,8192]{2,1,0:T(8,128)S(1)}, f32[4,12,8192]{2,1,0:T(8,128)}, u32[]{:S(2)}) copy-start(f32[4,12,8192]{2,1,0:T(8,128)} %copy-done) | copy-start | bytes 4718596
  120.1 7.0 %copy-start.8 = (f32[10,8192]{1,0:T(8,128)S(1)}, f32[10,8192]{1,0:T(8,128)}, u32[]{:S(2)}) copy-start(f32[10,8192]{1,0:T(8,128)} %copy-done.7) | copy-start | bytes 983044
  120.1 7.0 %copy-start.14 = (f32[10,8192]{1,0:T(8,128)S(1)}, f32[10,8192]{1,0:T(8,128)}, u32[]{:S(2)}) copy-start(f32[10,8192]{1,0:T(8,128)} %get-tuple-element.75) | copy-start | bytes 983044
  120.1 7.0 %copy-start.15 = (f32[10,8192]{1,0:T(8,128)S(1)}, f32[10,8192]{1,0:T(8,128)}, u32[]{:S(2)}) copy-start(f32[10,8192]{1,0:T(8,128)} %get-tuple-element.109) | copy-start | bytes 983044
  128.9 6.2 %collective-permute-start.8 = (f32[1,2,8192]{2,1,0:T(2,128)S(1)}, f32[1,2,8192]{2,1,0:T(2,128)S(1)}, u32[]{:S(2)}, u32[]{:S(2)}) collective-permute-start(f32[1,2,8192]{2,1,0:T(2,128)S(1)} %get-tuple-element.93), channel_id=1, source_target_pairs={{1,0},{2,1},{3,2},{4,3},{5,4},{6,5},{7,6},{8,7},{9,8},{10,9},{11,1... | collective-permute-start | bytes 196616 | tf_op jit(solution)/shard_map/ppermute | solution.py:12
  130.8 8.3 %collective-permute-start.9 = (f32[1,2,8192]{2,1,0:T(2,128)S(1)}, f32[1,2,8192]{2,1,0:T(2,128)S(1)}, u32[]{:S(2)}, u32[]{:S(2)}) collective-permute-start(f32[1,2,8192]{2,1,0:T(2,128)S(1)} %get-tuple-element.92), channel_id=1, source_target_pairs={{0,1},{1,2},{2,3},{3,4},{4,5},{5,6},{6,7},{7,8},{8,9},{9,10},{10,1... | collective-permute-start | bytes 196616 | tf_op jit(solution)/shard_map/ppermute | solution.py:12
  139.1 0.7 copy-start.22
Sparse Core Ops, SparseCore 0:
  140.0 69.2 all-reduce.29
where the time goes:
time: 218 us
  waiting for transfers between devices  98 us (45%)
  starting transfers between devices  61.7 us (28%)
  other arithmetic  28.1 us (13%)
  local copies, waits for them, and re-layouts  15.7 us (7%)
  between operations  14.1 us (6%)
    psum x1, waiting for transfers between devices, per_device(): total = lax.psum(local_grad, 'event')  69.4 us
    ppermute x3, starting transfers between devices, padded_2(): lax.ppermute(head, axis, [((i + 1) % count, i) for i in range(ends)])  19.6 us
    ppermute x4, starting transfers between devices, shifted(): lax.ppermute(value, axis, [(source, source + steps) for source in range(i...  14.4 us
    all_to_all x1, starting transfers between devices, per_device(): lax.all_to_all(send_cells.reshape(tile_count, capacity), 'tile', split_ax...  12.4 us
    ppermute x4, waiting for transfers between devices, shifted(): lax.ppermute(value, axis, [(source, source + steps) for source in range(i...  11.8 us
    all_to_all x1, waiting for transfers between devices, per_device(): lax.all_to_all(send_cells.reshape(tile_count, capacity), 'tile', split_ax...  10.1 us
    ppermute x3, starting transfers between devices, padded_2(): lax.ppermute(tail, axis, [(i, (i + 1) % count) for i in range(ends)])  9.78 us
    all_to_all x1, starting transfers between devices, per_device(): lax.all_to_all(send_values.reshape(tile_count, capacity), 'tile', split_a...  5.45 us
  transfers between devices with their start and end apart: 13, of which 9 were waited for; matrix products, arithmetic and copies ran while one was open for 6% of the time, Pallas kernels for 0%

commit v1 on v0

--- a/solution.py
+++ b/solution.py
@@ -155,7 +155,7 @@
             folded = fold_rims(jnp.stack((back_surface, back_east, back_north)), 2)
             sense_surface, sense_east, sense_north = (folded[0], folded[1], folded[2])
     local_grad = fold_rims(rough_sense[None], width)[0]
-    total = lax.psum(local_grad, "event")
+    total = jnp.sum(lax.all_gather(local_grad, "event"), axis=0)
     share = col_count // lax.axis_size("event")
     return lax.dynamic_slice_in_dim(total, lax.axis_index("event") * share, share, 1)
 

time: 218 us -> 178 us (0.82)
  the two profiles are of different devices: /device:TPU:2 before, /device:TPU:1 now
where the time goes in v1:
time: 178 us; the launch traced here: 177 us
  waiting for transfers between devices  68.8 us (39%)
  starting transfers between devices  49.2 us (28%)
  other arithmetic  29.8 us (17%)
  local copies, waits for them, and re-layouts  14.9 us (8%)
  between operations  14.1 us (8%)
    all_gather x1, waiting for transfers between devices, per_device(): total = jnp.sum(lax.all_gather(local_grad, 'event'), axis=0)  43.2 us
    all_to_all x1, starting transfers between devices, per_device(): lax.all_to_all(send_cells.reshape(tile_count, capacity), 'tile', split_ax...  19.9 us
    ppermute x4, starting transfers between devices, shifted(): lax.ppermute(value, axis, [(source, source + steps) for source in range(i...  11.2 us
    all_to_all x1, waiting for transfers between devices, per_device(): lax.all_to_all(send_cells.reshape(tile_count, capacity), 'tile', split_ax...  9.9 us
    ppermute x3, starting transfers between devices, padded_2(): lax.ppermute(tail, axis, [(i, (i + 1) % count) for i in range(ends)])  9.39 us
    all_to_all x1, waiting for transfers between devices, per_device(): lax.all_to_all(send_values.reshape(tile_count, capacity), 'tile', split_a...  6.53 us
    all_to_all x1, starting transfers between devices, per_device(): lax.all_to_all(send_values.reshape(tile_count, capacity), 'tile', split_a...  4.67 us
    ppermute x3, starting transfers between devices, padded_2(): lax.ppermute(head, axis, [((i + 1) % count, i) for i in range(ends)])  4.06 us
  transfers between devices with their start and end apart: 13, of which 8 were waited for; matrix products, arithmetic and copies ran while one was open for 7% of the time, Pallas kernels for 0%

profile of v1, /device:TPU:1, one launch (start us, length us, event | category | flops | bytes accessed | tf_op | source)
XLA Modules:
  0.0 176.9 jit_solution(5764286779834283115)
XLA Ops:
  6.5 1.4 pad_maximum_fusion.31
  7.9 4.4 %collective-permute-start = (f32[2,2,8192]{2,1,0:T(2,128)S(1)}, f32[2,2,8192]{2,1,0:T(2,128)S(1)}, u32[]{:S(2)}, u32[]{:S(2)}) collective-permute-start(f32[2,2,8192]{2,1,0:T(2,128)S(1)} %get-tuple-element.102), channel_id=1, source_target_pairs={{0,1},{1,2},{2,3},{3,4},{4,5},{5,6},{6,7},{7,8},{8,9},{9,10},{10,1... | collective-permute-start | bytes 393224 | tf_op jit(solution)/shard_map/ppermute | solution.py:23
  12.3 1.3 collective-permute-start.1
  13.6 0.7 fusion.43
  15.1 0.8 fusion.40
  16.6 1.6 scatter_custom_fusion
  18.1 0.7 all_to_all.12
  18.8 19.9 %all-to-all-start = ((s32[64,1,8]{2,1,0:T(1,128)}), s32[64,1,8]{2,1,0:T(1,128)S(1)}, u32[]{:S(2)}, u32[]{:S(2)}) async-start(s32[64,1,8]{2,1,0:T(1,128)} %bitcast.12), calls=%async_computation | async-start | bytes 65536 | tf_op jit(solution)/shard_map/all_to_all | solution.py:114
  38.8 1.1 convert_element_type.19
  39.9 1.6 scatter_custom_fusion.1
  41.5 0.7 all_to_all.14
  42.2 9.9 %all-to-all-done = s32[64,1,8]{2,1,0:T(1,128)S(1)} async-done(((s32[64,1,8]{2,1,0:T(1,128)}), s32[64,1,8]{2,1,0:T(1,128)S(1)}, u32[]{:S(2)}, u32[]{:S(2)}) %all-to-all-start) | async-done | bytes 2080 | tf_op jit(solution)/shard_map/all_to_all | solution.py:114
  52.1 4.7 %all-to-all-start.1 = ((f32[64,1,8]{2,1,0:T(1,128)}), f32[64,1,8]{2,1,0:T(1,128)S(1)}, u32[]{:S(2)}, u32[]{:S(2)}) async-start(f32[64,1,8]{2,1,0:T(1,128)} %bitcast.32), calls=%async_computation.1 | async-start | bytes 65536 | tf_op jit(solution)/shard_map/all_to_all | solution.py:121
  56.8 1.0 pad_maximum_fusion.27
  57.8 2.9 %collective-permute-start.2 = (f32[4,2,8192]{2,1,0:T(2,128)}, f32[4,2,8192]{2,1,0:T(2,128)S(1)}, u32[]{:S(2)}, u32[]{:S(2)}) collective-permute-start(f32[4,2,8192]{2,1,0:T(2,128)} %get-tuple-element.88), channel_id=1, source_target_pairs={{0,1},{1,2},{2,3},{3,4},{4,5},{5,6},{6,7},{7,8},{8,9},{9,10},{10,1... | collective-permute-start | bytes 786440 | tf_op jit(solution)/shard_map/ppermute | solution.py:23
  60.7 1.3 collective-permute-start.3
  62.6 0.7 reduce.18
  63.5 6.5 %all-to-all-done.1 = f32[64,1,8]{2,1,0:T(1,128)S(1)} async-done(((f32[64,1,8]{2,1,0:T(1,128)}), f32[64,1,8]{2,1,0:T(1,128)S(1)}, u32[]{:S(2)}, u32[]{:S(2)}) %all-to-all-start.1) | async-done | bytes 2080 | tf_op jit(solution)/shard_map/all_to_all | solution.py:121
  70.6 0.7 reduce.19
  71.4 1.3 pad_maximum_fusion.3
  73.4 0.7 copy-done.21
  74.5 2.0 %fusion.57 = (f32[10,8192]{1,0:T(8,128)S(1)}, f32[10,8192]{1,0:T(8,128)S(1)}, f32[10,8192]{1,0:T(8,128)}) fusion(f32[2,12,8192]{2,1,0:T(8,128)S(1)} %pad_maximum_fusion.3, f32[4,12,8192]{2,1,0:T(8,128)S(1)} %pad_maximum_fusion, f32[10,8192]{1,0:T(8,128)S(1)} %slice_bitcast_fusion.5), kind=kLoop, calls=%fused_computation.161 | loop fusion | flops 1392640 | bytes 2949120 | tf_op jit(solution)/shard_map/div | solution.py:54
  76.6 1.4 pad_slice_fusion.3
  78.3 2.1 %collective-permute-start.4 = (f32[4,2,8192]{2,1,0:T(2,128)S(1)}, f32[4,2,8192]{2,1,0:T(2,128)S(1)}, u32[]{:S(2)}, u32[]{:S(2)}) collective-permute-start(f32[4,2,8192]{2,1,0:T(2,128)S(1)} %get-tuple-element.86), channel_id=1, source_target_pairs={{0,1},{1,2},{2,3},{3,4},{4,5},{5,6},{6,7},{7,8},{8,9},{9,10},{10,1... | collective-permute-start | bytes 786440 | tf_op jit(solution)/shard_map/ppermute | solution.py:23
  80.4 1.5 collective-permute-start.5
  81.9 1.8 %collective-permute-done.4 = f32[4,2,8192]{2,1,0:T(2,128)S(1)} collective-permute-done((f32[4,2,8192]{2,1,0:T(2,128)S(1)}, f32[4,2,8192]{2,1,0:T(2,128)S(1)}, u32[]{:S(2)}, u32[]{:S(2)}) %collective-permute-start.4) | collective-permute-done | bytes 262176 | tf_op jit(solution)/shard_map/ppermute | solution.py:23
  83.7 3.8 %collective-permute-done.5 = f32[4,2,8192]{2,1,0:T(2,128)S(1)} collective-permute-done((f32[4,2,8192]{2,1,0:T(2,128)S(1)}, f32[4,2,8192]{2,1,0:T(2,128)S(1)}, u32[]{:S(2)}, u32[]{:S(2)}) %collective-permute-start.5) | collective-permute-done | bytes 262176 | tf_op jit(solution)/shard_map/ppermute | solution.py:25
  87.9 2.0 %fusion.54 = (f32[10,8192]{1,0:T(8,128)S(1)}, f32[10,8192]{1,0:T(8,128)}, f32[10,8192]{1,0:T(8,128)S(1)}) fusion(f32[10,8192]{1,0:T(8,128)S(1)} %slice_bitcast_fusion.1, f32[2,12,8192]{2,1,0:T(8,128)S(1)} %pad_maximum_fusion.3, f32[4,12,8192]{2,1,0:T(8,128)S(1)} %pad_maximum_fusion.1), kind=kLoop, calls=%fused_computation.159 | loop fusion | flops 1392640 | bytes 2949120 | tf_op jit(solution)/shard_map/div | solution.py:54
  90.3 1.1 fusion.55
  91.4 0.8 fusion.29
  92.2 1.0 copy.16
  93.2 3.1 %gather_fusion = f32[512]{0:T(512)S(1)} fusion(f32[65536]{0:T(1024)S(1)} %bitcast.242, s32[1024]{0:T(1024)S(1)} %pad_clamp_fusion), kind=kCustom, calls=%fused_computation | custom fusion | bytes 6144 | tf_op jit(solution)/shard_map/jit(_take)/gather | solution.py:131
  96.4 3.9 %scatter_custom_fusion.2 = f32[65536]{0:T(1024)} fusion(s32[512]{0:T(512)S(1)} %bitcast.254, f32[512]{0:T(512)S(1)} %subtract_select_fusion, f32[]{:T(128)} %constant.143.clone.1), kind=kCustom, calls=%fused_computation.127 | custom fusion | flops 512 | bytes 262148 | tf_op jit(solution)/shard_map/scatter-add | solution.py:136
  100.3 1.0 reshape.255
  101.4 1.3 fusion.52
  102.9 1.7 fusion
  104.7 0.7 add_add_fusion.1
  106.3 1.3 collective-permute-start.6
  107.8 4.1 %collective-permute-start.7 = (f32[3,2,8192]{2,1,0:T(2,128)S(1)}, f32[3,2,8192]{2,1,0:T(2,128)S(1)}, u32[]{:S(2)}, u32[]{:S(2)}) collective-permute-start(f32[3,2,8192]{2,1,0:T(2,128)S(1)} %get-tuple-element.84), channel_id=1, source_target_pairs={{0,1},{1,2},{2,3},{3,4},{4,5},{5,6},{6,7},{7,8},{8,9},{9,10},{10,1... | collective-permute-start | bytes 589832 | tf_op jit(solution)/shard_map/ppermute | solution.py:12
  111.9 0.8 collective-permute-done.6
  112.9 1.6 collective-permute-done.7
  114.9 1.5 fusion.1
  116.7 1.3 collective-permute-start.8
  118.0 4.4 %collective-permute-start.9 = (f32[1,2,8192]{2,1,0:T(2,128)S(1)}, f32[1,2,8192]{2,1,0:T(2,128)S(1)}, u32[]{:S(2)}, u32[]{:S(2)}) collective-permute-start(f32[1,2,8192]{2,1,0:T(2,128)S(1)} %get-tuple-element.92), channel_id=1, source_target_pairs={{0,1},{1,2},{2,3},{3,4},{4,5},{5,6},{6,7},{7,8},{8,9},{9,10},{10,1... | collective-permute-start | bytes 196616 | tf_op jit(solution)/shard_map/ppermute | solution.py:12
  122.5 1.2 collective-permute-done.9
  123.8 0.7 copy-done.18
  124.5 43.2 %all-gather.2.cloned.1.call-done = f32[8,8,8192]{2,1,0:T(8,128)} async-done(((f32[1,8,8192]{2,1,0:T(8,128)}), f32[8,8,8192]{2,1,0:T(8,128)}) %all-gather.2.cloned.1.call-update) | async-done | bytes 2097168 | tf_op jit(solution)/shard_map/all_gather | solution.py:158
  167.7 1.7 reduce_sum.22
  (95 shorter events, 8.0 us)
Async XLA Ops:
  6.5 50.3 %copy-start.9 = (f32[1,8,8192]{2,1,0:T(8,128)S(1)}, f32[1,8,8192]{2,1,0:T(8,128)}, u32[]{:S(2)}) copy-start(f32[1,8,8192]{2,1,0:T(8,128)} %param.18) | copy-start | bytes 786436
  6.5 50.3 %copy-start.12 = (f32[1,8,8192]{2,1,0:T(8,128)S(1)}, f32[1,8,8192]{2,1,0:T(8,128)}, u32[]{:S(2)}) copy-start(f32[1,8,8192]{2,1,0:T(8,128)} %param.19) | copy-start | bytes 786436
  6.5 50.3 %copy-start.10 = (f32[1,8,8192]{2,1,0:T(8,128)S(1)}, f32[1,8,8192]{2,1,0:T(8,128)}, u32[]{:S(2)}) copy-start(f32[1,8,8192]{2,1,0:T(8,128)} %param.20) | copy-start | bytes 786436
  7.9 63.5 %collective-permute-start = (f32[2,2,8192]{2,1,0:T(2,128)S(1)}, f32[2,2,8192]{2,1,0:T(2,128)S(1)}, u32[]{:S(2)}, u32[]{:S(2)}) collective-permute-start(f32[2,2,8192]{2,1,0:T(2,128)S(1)} %get-tuple-element.102), channel_id=1, source_target_pairs={{0,1},{1,2},{2,3},{3,4},{4,5},{5,6},{6,7},{7,8},{8,9},{9,10},{10,1... | collective-permute-start | bytes 393224 | tf_op jit(solution)/shard_map/ppermute | solution.py:23
  12.3 59.1 %collective-permute-start.1 = (f32[2,2,8192]{2,1,0:T(2,128)S(1)}, f32[2,2,8192]{2,1,0:T(2,128)}, u32[]{:S(2)}, u32[]{:S(2)}) collective-permute-start(f32[2,2,8192]{2,1,0:T(2,128)S(1)} %get-tuple-element.103), channel_id=1, source_target_pairs={{1,0},{2,1},{3,2},{4,3},{5,4},{6,5},{7,6},{8,7},{9,8},{10,9},{11,1... | collective-permute-start | bytes 393224 | tf_op jit(solution)/shard_map/ppermute | solution.py:25
  18.8 33.2 %all-to-all-start = ((s32[64,1,8]{2,1,0:T(1,128)}), s32[64,1,8]{2,1,0:T(1,128)S(1)}, u32[]{:S(2)}, u32[]{:S(2)}) async-start(s32[64,1,8]{2,1,0:T(1,128)} %bitcast.12), calls=%async_computation | async-start | bytes 65536 | tf_op jit(solution)/shard_map/all_to_all | solution.py:114
  39.9 38.1 %copy-start.2 = (f32[1,2,8,8192]{3,2,1,0:T(8,128)}, f32[1,2,8,8192]{3,2,1,0:T(8,128)S(1)}, u32[]{:S(2)}) copy-start(f32[1,2,8,8192]{3,2,1,0:T(8,128)S(1)} %convert_element_type.19) | copy-start | bytes 1572868
  52.1 18.0 %all-to-all-start.1 = ((f32[64,1,8]{2,1,0:T(1,128)}), f32[64,1,8]{2,1,0:T(1,128)S(1)}, u32[]{:S(2)}, u32[]{:S(2)}) async-start(f32[64,1,8]{2,1,0:T(1,128)} %bitcast.32), calls=%async_computation.1 | async-start | bytes 65536 | tf_op jit(solution)/shard_map/all_to_all | solution.py:121
  56.7 111.0 %all-gather.2.cloned.1.call-start = ((), (), s32[]{:S(2)}) async-start(), calls=%async_computation.2 | async-start | bytes 2359296 | tf_op jit(solution)/shard_map/all_gather | solution.py:158
  57.8 14.9 %collective-permute-start.2 = (f32[4,2,8192]{2,1,0:T(2,128)}, f32[4,2,8192]{2,1,0:T(2,128)S(1)}, u32[]{:S(2)}, u32[]{:S(2)}) collective-permute-start(f32[4,2,8192]{2,1,0:T(2,128)} %get-tuple-element.88), channel_id=1, source_target_pairs={{0,1},{1,2},{2,3},{3,4},{4,5},{5,6},{6,7},{7,8},{8,9},{9,10},{10,1... | collective-permute-start | bytes 786440 | tf_op jit(solution)/shard_map/ppermute | solution.py:23
  60.7 12.0 %collective-permute-start.3 = (f32[4,2,8192]{2,1,0:T(2,128)}, f32[4,2,8192]{2,1,0:T(2,128)S(1)}, u32[]{:S(2)}, u32[]{:S(2)}) collective-permute-start(f32[4,2,8192]{2,1,0:T(2,128)} %get-tuple-element.89), channel_id=1, source_target_pairs={{1,0},{2,1},{3,2},{4,3},{5,4},{6,5},{7,6},{8,7},{9,8},{10,9},{11,1... | collective-permute-start | bytes 786440 | tf_op jit(solution)/shard_map/ppermute | solution.py:25
  72.7 0.7 copy-start.19
  73.4 0.7 copy-start.21
  74.4 2.1 %copy-start = (f32[4,12,8192]{2,1,0:T(8,128)}, f32[4,12,8192]{2,1,0:T(8,128)S(1)}, u32[]{:S(2)}) copy-start(f32[4,12,8192]{2,1,0:T(8,128)S(1)} %pad_maximum_fusion) | copy-start | bytes 4718596
  74.5 2.1 %copy-start.11 = (f32[1,8,8192]{2,1,0:T(8,128)S(1)}, f32[1,8,8192]{2,1,0:T(8,128)}, u32[]{:S(2)}) copy-start(f32[1,8,8192]{2,1,0:T(8,128)} %param.20) | copy-start | bytes 786436
  74.5 2.1 %copy-start.13 = (f32[1,8,8192]{2,1,0:T(8,128)S(1)}, f32[1,8,8192]{2,1,0:T(8,128)}, u32[]{:S(2)}) copy-start(f32[1,8,8192]{2,1,0:T(8,128)} %param.19) | copy-start | bytes 786436
  74.5 2.1 %copy-start.20 = (f32[4,2,8192]{2,1,0:T(2,128)S(1)}, f32[4,2,8192]{2,1,0:T(2,128)}, u32[]{:S(2)}) copy-start(f32[4,2,8192]{2,1,0:T(2,128)} %copy-done.19) | copy-start | bytes 786436
  74.5 2.1 %copy-start.22 = (f32[4,2,8192]{2,1,0:T(2,128)S(1)}, f32[4,2,8192]{2,1,0:T(2,128)}, u32[]{:S(2)}) copy-start(f32[4,2,8192]{2,1,0:T(2,128)} %copy-done.21) | copy-start | bytes 786436
  76.5 1.5 copy-start.7
  78.3 5.4 %collective-permute-start.4 = (f32[4,2,8192]{2,1,0:T(2,128)S(1)}, f32[4,2,8192]{2,1,0:T(2,128)S(1)}, u32[]{:S(2)}, u32[]{:S(2)}) collective-permute-start(f32[4,2,8192]{2,1,0:T(2,128)S(1)} %get-tuple-element.86), channel_id=1, source_target_pairs={{0,1},{1,2},{2,3},{3,4},{4,5},{5,6},{6,7},{7,8},{8,9},{9,10},{10,1... | collective-permute-start | bytes 786440 | tf_op jit(solution)/shard_map/ppermute | solution.py:23
  80.4 7.1 %collective-permute-start.5 = (f32[4,2,8192]{2,1,0:T(2,128)S(1)}, f32[4,2,8192]{2,1,0:T(2,128)S(1)}, u32[]{:S(2)}, u32[]{:S(2)}) collective-permute-start(f32[4,2,8192]{2,1,0:T(2,128)S(1)} %get-tuple-element.87), channel_id=1, source_target_pairs={{1,0},{2,1},{3,2},{4,3},{5,4},{6,5},{7,6},{8,7},{9,8},{10,9},{11,1... | collective-permute-start | bytes 786440 | tf_op jit(solution)/shard_map/ppermute | solution.py:25
  89.9 1.4 copy-start.5
  90.3 1.1 copy-start.3
  101.3 1.4 copy-start.6
  101.3 1.4 copy-start.16
  101.3 1.6 copy-start.17
  106.3 6.4 %collective-permute-start.6 = (f32[3,2,8192]{2,1,0:T(2,128)S(1)}, f32[3,2,8192]{2,1,0:T(2,128)S(1)}, u32[]{:S(2)}, u32[]{:S(2)}) collective-permute-start(f32[3,2,8192]{2,1,0:T(2,128)S(1)} %get-tuple-element.85), channel_id=1, source_target_pairs={{1,0},{2,1},{3,2},{4,3},{5,4},{6,5},{7,6},{8,7},{9,8},{10,9},{11,1... | collective-permute-start | bytes 589832 | tf_op jit(solution)/shard_map/ppermute | solution.py:12
  107.7 7.0 %copy-start.4 = (f32[1,2,8,8192]{3,2,1,0:T(8,128)S(1)}, f32[1,2,8,8192]{3,2,1,0:T(8,128)}, u32[]{:S(2)}) copy-start(f32[1,2,8,8192]{3,2,1,0:T(8,128)} %copy-done.2) | copy-start | bytes 1572868
  107.8 6.7 %collective-permute-start.7 = (f32[3,2,8192]{2,1,0:T(2,128)S(1)}, f32[3,2,8192]{2,1,0:T(2,128)S(1)}, u32[]{:S(2)}, u32[]{:S(2)}) collective-permute-start(f32[3,2,8192]{2,1,0:T(2,128)S(1)} %get-tuple-element.84), channel_id=1, source_target_pairs={{0,1},{1,2},{2,3},{3,4},{4,5},{5,6},{6,7},{7,8},{8,9},{9,10},{10,1... | collective-permute-start | bytes 589832 | tf_op jit(solution)/shard_map/ppermute | solution.py:12
  112.9 2.0 %copy-start.1 = (f32[4,12,8192]{2,1,0:T(8,128)S(1)}, f32[4,12,8192]{2,1,0:T(8,128)}, u32[]{:S(2)}) copy-start(f32[4,12,8192]{2,1,0:T(8,128)} %copy-done) | copy-start | bytes 4718596
  112.9 2.0 %copy-start.8 = (f32[10,8192]{1,0:T(8,128)S(1)}, f32[10,8192]{1,0:T(8,128)}, u32[]{:S(2)}) copy-start(f32[10,8192]{1,0:T(8,128)} %copy-done.7) | copy-start | bytes 983044
  112.9 2.0 %copy-start.14 = (f32[10,8192]{1,0:T(8,128)S(1)}, f32[10,8192]{1,0:T(8,128)}, u32[]{:S(2)}) copy-start(f32[10,8192]{1,0:T(8,128)} %get-tuple-element.75) | copy-start | bytes 983044
  112.9 2.0 %copy-start.15 = (f32[10,8192]{1,0:T(8,128)S(1)}, f32[10,8192]{1,0:T(8,128)}, u32[]{:S(2)}) copy-start(f32[10,8192]{1,0:T(8,128)} %get-tuple-element.109) | copy-start | bytes 983044
  116.7 5.8 %collective-permute-start.8 = (f32[1,2,8192]{2,1,0:T(2,128)S(1)}, f32[1,2,8192]{2,1,0:T(2,128)S(1)}, u32[]{:S(2)}, u32[]{:S(2)}) collective-permute-start(f32[1,2,8192]{2,1,0:T(2,128)S(1)} %get-tuple-element.93), channel_id=1, source_target_pairs={{1,0},{2,1},{3,2},{4,3},{5,4},{6,5},{7,6},{8,7},{9,8},{10,9},{11,1... | collective-permute-start | bytes 196616 | tf_op jit(solution)/shard_map/ppermute | solution.py:12
  118.0 5.8 %collective-permute-start.9 = (f32[1,2,8192]{2,1,0:T(2,128)S(1)}, f32[1,2,8192]{2,1,0:T(2,128)S(1)}, u32[]{:S(2)}, u32[]{:S(2)}) collective-permute-start(f32[1,2,8192]{2,1,0:T(2,128)S(1)} %get-tuple-element.92), channel_id=1, source_target_pairs={{0,1},{1,2},{2,3},{3,4},{4,5},{5,6},{6,7},{7,8},{8,9},{9,10},{10,1... | collective-permute-start | bytes 196616 | tf_op jit(solution)/shard_map/ppermute | solution.py:12
  123.8 0.7 copy-start.18
Sparse Core Ops, SparseCore 0:
  124.7 43.0 all-gather.1
